TPU v7x, 512 devices: a whole 4x8x8 slice. The times are simulated.
512 devices in a mesh: ctx: 16 (over y, core), head: 32 (over z, x).
Axes of the slice: x: 4, y: 8, z: 8, core: 2. Of those that a mesh axis runs over, the one named last changes fastest.
Arguments:
- query_rows: bfloat16 [6144, 64, 128], P('ctx', 'head'), may hold values from -1.75 to 1.75
- key_matrix: bfloat16 [6144, 64, 128], P('ctx', 'head'), may hold values from -1.75 to 1.75
- value_rows: bfloat16 [6144, 64, 128], P('ctx', 'head'), may hold values from -55 to 55
- decay_log: float32 [6144, 64], P('ctx', 'head'), may hold values from -0.6 to 0
- norm_gain: float32 [64, 128], P('head'), may hold values from 0.1 to 1.9
- grad_out: bfloat16 [6144, 64, 128], P('ctx', 'head'), may hold values from -6 to 6
Outputs:
- output: bfloat16 [6144, 64, 128], P('ctx', 'head')
- grad_query: bfloat16 [6144, 64, 128], P('ctx', 'head')
- grad_key: bfloat16 [6144, 64, 128], P('ctx', 'head')
- grad_value: bfloat16 [6144, 64, 128], P('ctx', 'head')
All inputs are finite; a program needn't handle non-finite values.
Results may differ from a plain program's by a relative error of at most 0.019.
Values sent between devices are 32-bit elements; how exact they have to be, the bound alone decides.
A program may use at most 64 MiB of HBM per device.

v0:
```python
import jax
import jax.numpy as jnp
from jax import lax
from jax.sharding import PartitionSpec as P

GROUP = 128
epsilon = 1e-06


def weigh_gathered(gathered, log_rates, position, forward):
    device_ranks = jnp.arange(log_rates.shape[0], dtype=jnp.int32)
    running = jnp.cumsum(log_rates, axis=0)
    own_total = running[position]
    if forward:
        keep_mask = device_ranks < position
        spread = (own_total - log_rates[position])[None, :] - running
    else:
        keep_mask = device_ranks > position
        spread = running - log_rates - own_total[None, :]
    keep_mask = keep_mask[:, None]
    factors = jnp.where(keep_mask, jnp.exp(jnp.where(keep_mask, spread, 0.0)), 0.0)
    return jnp.einsum("nh,nhde->hde", factors, gathered, precision=lax.Precision.HIGHEST)


def per_device(query_rows, key_matrix, value_rows, decay_log, norm_gain, grad_out):
    token_count, head_count, head_size = query_rows.shape
    num_blocks = token_count // GROUP
    query_blocks = query_rows.reshape(num_blocks, GROUP, head_count, head_size)
    key_blocks = key_matrix.reshape(num_blocks, GROUP, head_count, head_size)
    value_blocks = value_rows.reshape(num_blocks, GROUP, head_count, head_size)
    cumulative = jnp.cumsum(decay_log.reshape(num_blocks, GROUP, head_count), axis=1)
    block_total = cumulative[:, -1, :]
    cum_major = jnp.transpose(cumulative, (0, 2, 1))
    row_ids = lax.broadcasted_iota(jnp.int32, (GROUP, GROUP), 0)
    col_ids = lax.broadcasted_iota(jnp.int32, (GROUP, GROUP), 1)
    causal = (row_ids >= col_ids)[None, None]
    spread = cum_major[:, :, :, None] - cum_major[:, :, None, :]
    mask_weight = jnp.where(causal, jnp.exp(jnp.where(causal, spread, 0.0)), 0.0)
    scores = jnp.einsum(
        "cihd,cjhd->chij", query_blocks, key_blocks, preferred_element_type=jnp.float32
    )
    attn_weights = (scores * mask_weight).astype(jnp.bfloat16)
    local_part = jnp.einsum(
        "chij,cjhd->cihd", attn_weights, value_blocks, preferred_element_type=jnp.float32
    )

    def advance(carry_state, pieces):
        key_part, value_part, cum_part, total_part = pieces
        decayed = (key_part * jnp.exp(total_part[None, :] - cum_part)[:, :, None]).astype(
            jnp.bfloat16
        )
        fresh_term = jnp.einsum(
            "ihd,ihe->hde", decayed, value_part, preferred_element_type=jnp.float32
        )
        return (jnp.exp(total_part)[:, None, None] * carry_state + fresh_term, carry_state)

    zero_state = jnp.zeros((head_count, head_size, head_size), jnp.float32)
    end_state, local_states = lax.scan(
        advance, zero_state, (key_blocks, value_blocks, cumulative, block_total)
    )
    total_log = jnp.sum(block_total, axis=0)
    position = lax.axis_index("ctx")
    gathered, log_rates = (
        lax.all_gather(end_state[None], "ctx", axis=0, tiled=True),
        lax.all_gather(total_log[None], "ctx", axis=0, tiled=True),
    )
    incoming = weigh_gathered(gathered, log_rates, position, True)
    before = jnp.cumsum(block_total, axis=0) - block_total
    state_bf = (local_states + jnp.exp(before)[:, :, None, None] * incoming[None]).astype(
        jnp.bfloat16
    )
    carried_part = (
        jnp.einsum("cihd,chde->cihe", query_blocks, state_bf, preferred_element_type=jnp.float32)
        * jnp.exp(cumulative)[:, :, :, None]
    )
    attention = (
        (local_part + carried_part).astype(jnp.bfloat16).reshape(token_count, head_count, head_size)
    )
    attn_f = attention.astype(jnp.float32)
    grad_f = grad_out.astype(jnp.float32)
    features = head_count * lax.axis_size("head") * head_size
    square_sum = lax.psum(jnp.sum(attn_f * attn_f, axis=(1, 2)), "head")
    inv_rms = lax.rsqrt(square_sum / features + epsilon)
    output = (attn_f * inv_rms[:, None, None] * norm_gain[None]).astype(jnp.bfloat16)
    scaled_grad = norm_gain[None] * (grad_f + output.astype(jnp.float32))
    inner = lax.psum(jnp.sum(scaled_grad * attn_f, axis=(1, 2)), "head")
    grad_attention = (
        inv_rms[:, None, None] * scaled_grad
        - attn_f * (inv_rms**3 * inner / features)[:, None, None]
    ).astype(jnp.bfloat16)
    grad_blocks = grad_attention.reshape(num_blocks, GROUP, head_count, head_size)
    grad_dots = jnp.einsum(
        "cihe,cjhe->chij", grad_blocks, value_blocks, preferred_element_type=jnp.float32
    )
    grad_scores = (grad_dots * mask_weight).astype(jnp.bfloat16)
    query_local = jnp.einsum(
        "chij,cjhd->cihd", grad_scores, key_blocks, preferred_element_type=jnp.float32
    )
    key_local = jnp.einsum(
        "chij,cihd->cjhd", grad_scores, query_blocks, preferred_element_type=jnp.float32
    )
    value_local = jnp.einsum(
        "chij,cihe->cjhe", attn_weights, grad_blocks, preferred_element_type=jnp.float32
    )
    query_carried = (
        jnp.einsum("cihe,chde->cihd", grad_blocks, state_bf, preferred_element_type=jnp.float32)
        * jnp.exp(cumulative)[:, :, :, None]
    )

    def retreat(carry_state, pieces):
        query_part, grad_part, cum_part, total_part = pieces
        decayed = (query_part * jnp.exp(cum_part)[:, :, None]).astype(jnp.bfloat16)
        fresh_term = jnp.einsum(
            "ihd,ihe->hde", decayed, grad_part, preferred_element_type=jnp.float32
        )
        return (jnp.exp(total_part)[:, None, None] * carry_state + fresh_term, carry_state)

    start_state, local_back = lax.scan(
        retreat, zero_state, (query_blocks, grad_blocks, cumulative, block_total), reverse=True
    )
    gathered_back, log_back = (
        lax.all_gather(start_state[None], "ctx", axis=0, tiled=True),
        lax.all_gather(total_log[None], "ctx", axis=0, tiled=True),
    )
    arriving = weigh_gathered(gathered_back, log_back, position, False)
    after = total_log[None, :] - jnp.cumsum(block_total, axis=0)
    back_bf = (local_back + jnp.exp(after)[:, :, None, None] * arriving[None]).astype(jnp.bfloat16)
    tail = jnp.exp(block_total[:, None, :] - cumulative)[:, :, :, None]
    key_carried = (
        jnp.einsum("cihe,chde->cihd", value_blocks, back_bf, preferred_element_type=jnp.float32)
        * tail
    )
    value_carried = (
        jnp.einsum("cihd,chde->cihe", key_blocks, back_bf, preferred_element_type=jnp.float32)
        * tail
    )
    shape_out = (token_count, head_count, head_size)
    grad_query = (query_local + query_carried).astype(jnp.bfloat16).reshape(shape_out)
    grad_key = (key_local + key_carried).astype(jnp.bfloat16).reshape(shape_out)
    grad_value = (value_local + value_carried).astype(jnp.bfloat16).reshape(shape_out)
    return (output, grad_query, grad_key, grad_value)


def solution(mesh):
    placed = (
        P("ctx", "head", None),
        P("ctx", "head", None),
        P("ctx", "head", None),
        P("ctx", "head"),
        P("head", None),
        P("ctx", "head", None),
    )
    return jax.shard_map(
        per_device,
        mesh=mesh,
        in_specs=placed,
        out_specs=(
            P("ctx", "head", None),
            P("ctx", "head", None),
            P("ctx", "head", None),
            P("ctx", "head", None),
        ),
        check_vma=False,
    )
```

profile of v0, /device:TPU:1, one launch (start us, length us, event | category | flops | bytes accessed | tf_op | source)
XLA Modules:
  0.0 262.6 jit_solution(10493295506692607835)
XLA Ops:
  7.2 0.8 copy.129
  8.0 0.2 reduce_window_sum.35
  8.6 1.0 copy.79
  9.5 1.0 copy.85
  10.6 1.4 while.30
  12.0 0.6 copy-done.1
  12.9 1.3 dynamic-slice
  14.9 0.2 dynamic-update-slice
  15.1 29.7 %all-reduce = f32[32]{0:T(128)S(1)} all-reduce(f32[32]{0:T(128)S(1)} %dynamic-update-slice), channel_id=2, replica_groups=mesh['ctx'=16,'head'=32] {'ctx'}, use_global_device_ids=true, to_apply=%add | all-reduce | flops 32 | bytes 256
  45.6 0.3 fusion.34
  45.9 14.7 %all-gather.6.cloned.1.call-done = f32[32,128,128]{2,1,0:T(8,128)} async-done(((f32[2,128,128]{2,1,0:T(8,128)}), f32[32,128,128]{2,1,0:T(8,128)}) %all-gather.6.cloned.1.call-update) | async-done | bytes 2097168 | tf_op jit(solution)/shard_map/all_gather | solution.py:64
  60.6 3.8 %fusion.24 = f32[2,1,128,128]{3,1,2,0:T(1,128)S(1)} fusion(f32[16,2,1,1]{0,2,3,1:T(1,128)S(1)} %copy.121, f32[16,2,128,128]{3,2,1,0:T(8,128)} %bitcast.159), kind=kOutput, calls=%fused_computation.34 | convolution fusion | flops 6291456 | bytes 2228352 | tf_op jit(solution)/shard_map/nh,nhde->hde/dot_general | solution.py:22
  64.4 0.3 fusion.27
  64.6 0.3 multiply_reduce_fusion
  65.0 61.6 %psum.14 = f32[384]{0:T(512)S(1)} all-reduce(f32[384]{0:T(512)S(1)} %bitcast.171), channel_id=1, replica_groups=mesh['ctx'=16,'head'=32] {'head'}, use_global_device_ids=true, to_apply=%region_7.8 | all-reduce | flops 384 | bytes 3072 | tf_op jit(solution)/shard_map/psum | solution.py:82
  126.6 0.2 fusion.43
  126.9 56.2 %psum.15 = f32[384]{0:T(512)S(1)} all-reduce(f32[384]{0:T(512)S(1)} %fusion.43), channel_id=1, replica_groups=mesh['ctx'=16,'head'=32] {'head'}, use_global_device_ids=true, to_apply=%region_9.10 | all-reduce | flops 384 | bytes 3072 | tf_op jit(solution)/shard_map/psum | solution.py:86
  183.1 0.2 fusion.45
  183.4 1.2 while.31
  184.6 0.6 copy-done
  185.6 0.9 copy.117
  186.5 0.3 fusion.37
  186.7 0.3 fusion.31
  187.3 0.9 copy.118
  188.2 60.8 %all-gather.8.cloned.1.call-done = f32[32,128,128]{2,1,0:T(8,128)} async-done(((f32[2,128,128]{2,1,0:T(8,128)}), f32[32,128,128]{2,1,0:T(8,128)}) %all-gather.8.cloned.1.call-update) | async-done | bytes 2097168 | tf_op jit(solution)/shard_map/all_gather | solution.py:122
  249.0 3.8 %fusion.22 = f32[2,1,128,128]{3,1,2,0:T(1,128)S(1)} fusion(f32[16,2,1,1]{0,2,3,1:T(1,128)S(1)} %copy.125, f32[16,2,128,128]{3,2,1,0:T(8,128)} %bitcast.160), kind=kOutput, calls=%fused_computation.32 | convolution fusion | flops 6291456 | bytes 2228352 | tf_op jit(solution)/shard_map/nh,nhde->hde/dot_general | solution.py:22
  252.8 0.3 fusion.29
  253.1 0.3 fusion.26
  253.4 0.3 fusion.39
  253.7 0.9 copy.119
  254.6 0.3 fusion.40
  254.9 0.9 copy.120
  (83 shorter events, 4.3 us)
Async XLA Ops:
  7.2 53.4 %all-gather.6.cloned.1.call-start = ((), (), s32[]{:S(2)}) async-start(), calls=%async_computation | async-start | bytes 2228224 | tf_op jit(solution)/shard_map/all_gather | solution.py:64
  10.6 2.3 copy-start.3
  12.0 0.7 copy-start.1
  12.6 236.4 %all-gather.8.cloned.1.call-start = ((), (), s32[]{:S(2)}) async-start(), calls=%async_computation.1 | async-start | bytes 2228224 | tf_op jit(solution)/shard_map/all_gather | solution.py:122
  64.3 62.3 %copy-start.2 = (bf16[384,2,128]{2,1,0:T(2,128)(2,1)S(1)}, bf16[384,2,128]{2,1,0:T(2,128)(2,1)}, u32[]{:S(2)}) copy-start(bf16[384,2,128]{2,1,0:T(2,128)(2,1)} %param.15) | copy-start | bytes 589828
  64.4 62.3 %copy-start.4 = (f32[2,128]{1,0:T(2,128)S(1)}, f32[2,128]{1,0:T(2,128)}, u32[]{:S(2)}) copy-start(f32[2,128]{1,0:T(2,128)} %param.14) | copy-start | bytes 3076
  184.6 0.7 copy-start
Sparse Core Ops, SparseCore 0:
  12.8 47.7 all-gather.5
  185.4 63.5 all-gather.7
where the time goes:
time: 263 us
  blocking collectives  148 us (56%)
  waiting for transfers between devices  75.5 us (29%)
  between operations  15 us (6%)
  matrix products  11.3 us (4%)
  local copies, waits for them, and re-layouts  11.2 us (4%)
    psum x1, blocking collectives, per_device(): square_sum = lax.psum(jnp.sum(attn_f * attn_f, axis=(1, 2)), 'head')  61.6 us
    all_gather x1, waiting for transfers between devices, per_device(): lax.all_gather(start_state[None], 'ctx', axis=0, tiled=True)  60.8 us
    psum x1, blocking collectives, per_device(): inner = lax.psum(jnp.sum(scaled_grad * attn_f, axis=(1, 2)), 'head')  56.2 us
    unnamed x1, blocking collectives  29.7 us
    all_gather x1, waiting for transfers between devices, per_device(): lax.all_gather(end_state[None], 'ctx', axis=0, tiled=True)  14.7 us
    unnamed x22, local copies, waits for them, and re-layouts  8.56 us
    dot_general x2, matrix products, weigh_gathered(): jnp.einsum('nh,nhde->hde', factors, gathered, precision=lax.Precision.HIG...  7.53 us
  transfers between devices with their start and end apart: 2, of which 2 were waited for; matrix products, arithmetic and copies ran while one was open for 2% of the time, Pallas kernels for 0%

commit v1 on v0

--- a/solution.py
+++ b/solution.py
@@ -2,6 +2,7 @@
 import jax.numpy as jnp
 from jax import lax
 from jax.sharding import PartitionSpec as P
+from jax.lax import all_gather
 
 GROUP = 128
 epsilon = 1e-06
@@ -23,6 +24,10 @@
 
 
 def per_device(query_rows, key_matrix, value_rows, decay_log, norm_gain, grad_out):
+
+    def search_seats_all_over_axis(array_here):
+        return jnp.sum(all_gather(array_here, "head"), axis=0)
+
     token_count, head_count, head_size = query_rows.shape
     num_blocks = token_count // GROUP
     query_blocks = query_rows.reshape(num_blocks, GROUP, head_count, head_size)
@@ -83,7 +88,7 @@
     inv_rms = lax.rsqrt(square_sum / features + epsilon)
     output = (attn_f * inv_rms[:, None, None] * norm_gain[None]).astype(jnp.bfloat16)
     scaled_grad = norm_gain[None] * (grad_f + output.astype(jnp.float32))
-    inner = lax.psum(jnp.sum(scaled_grad * attn_f, axis=(1, 2)), "head")
+    inner = search_seats_all_over_axis(jnp.sum(scaled_grad * attn_f, axis=(1, 2)))
     grad_attention = (
         inv_rms[:, None, None] * scaled_grad
         - attn_f * (inv_rms**3 * inner / features)[:, None, None]

time: 263 us -> 239 us (0.909)
  blocking collectives: 148 us -> 123 us
    psum x1 -> x0, blocking collectives: 56.2 us -> none  [per_device(): inner = lax.psum(jnp.sum(scaled_grad * attn_f, axis=(1, 2)), 'head')]
    all_gather x0 -> x1, blocking collectives: none -> 31.7 us  [search_seats_all_over_axis(): return jnp.sum(all_gather(array_here, 'head'), axis=0)]
    unnamed x22 -> x23, local copies, waits for them, and re-layouts: 8.56 us -> 8.57 us
where the time goes in v1:
time: 239 us; the launch traced here: 238 us
  blocking collectives  123 us (51%)
  waiting for transfers between devices  75.9 us (32%)
  between operations  15 us (6%)
  matrix products  11.3 us (5%)
  local copies, waits for them, and re-layouts  11.2 us (5%)
    psum x1, blocking collectives, per_device(): square_sum = lax.psum(jnp.sum(attn_f * attn_f, axis=(1, 2)), 'head')  61.6 us
    all_gather x1, waiting for transfers between devices, per_device(): lax.all_gather(start_state[None], 'ctx', axis=0, tiled=True)  61.2 us
    all_gather x1, blocking collectives, search_seats_all_over_axis(): return jnp.sum(all_gather(array_here, 'head'), axis=0)  31.7 us
    unnamed x1, blocking collectives  29.7 us
    all_gather x1, waiting for transfers between devices, per_device(): lax.all_gather(end_state[None], 'ctx', axis=0, tiled=True)  14.7 us
    unnamed x23, local copies, waits for them, and re-layouts  8.57 us
    dot_general x2, matrix products, weigh_gathered(): jnp.einsum('nh,nhde->hde', factors, gathered, precision=lax.Precision.HIG...  7.53 us
  transfers between devices with their start and end apart: 2, of which 2 were waited for; matrix products, arithmetic and copies ran while one was open for 2% of the time, Pallas kernels for 0%

profile of v1, /device:TPU:1, one launch (start us, length us, event | category | flops | bytes accessed | tf_op | source)
XLA Modules:
  0.0 238.5 jit_solution(4066593170136700170)
XLA Ops:
  7.2 0.8 copy.129
  8.0 0.2 reduce_window_sum.35
  8.6 1.0 copy.79
  9.5 1.0 copy.85
  10.6 1.4 while.30
  12.0 0.6 copy-done.1
  12.9 1.3 dynamic-slice
  14.9 0.2 dynamic-update-slice
  15.1 29.7 %all-reduce = f32[32]{0:T(128)S(1)} all-reduce(f32[32]{0:T(128)S(1)} %dynamic-update-slice), channel_id=2, replica_groups=mesh['ctx'=16,'head'=32] {'ctx'}, use_global_device_ids=true, to_apply=%add | all-reduce | flops 32 | bytes 256
  45.6 0.3 fusion.34
  45.9 14.7 %all-gather.8.cloned.1.call-done = f32[32,128,128]{2,1,0:T(8,128)} async-done(((f32[2,128,128]{2,1,0:T(8,128)}), f32[32,128,128]{2,1,0:T(8,128)}) %all-gather.8.cloned.1.call-update) | async-done | bytes 2097168 | tf_op jit(solution)/shard_map/all_gather | solution.py:69
  60.6 3.8 %fusion.24 = f32[2,1,128,128]{3,1,2,0:T(1,128)S(1)} fusion(f32[16,2,1,1]{0,2,3,1:T(1,128)S(1)} %copy.121, f32[16,2,128,128]{3,2,1,0:T(8,128)} %bitcast.159), kind=kOutput, calls=%fused_computation.34 | convolution fusion | flops 6291456 | bytes 2228352 | tf_op jit(solution)/shard_map/nh,nhde->hde/dot_general | solution.py:23
  64.4 0.3 fusion.27
  64.6 0.3 multiply_reduce_fusion
  65.0 61.6 %psum.7 = f32[384]{0:T(512)S(1)} all-reduce(f32[384]{0:T(512)S(1)} %bitcast.171), channel_id=1, replica_groups=mesh['ctx'=16,'head'=32] {'head'}, use_global_device_ids=true, to_apply=%region_7.8 | all-reduce | flops 384 | bytes 3072 | tf_op jit(solution)/shard_map/psum | solution.py:87
  126.6 0.2 fusion.43
  126.9 31.7 %all-gather.4 = f32[32,1,384]{2,1,0:T(1,128)S(1)} all-gather(f32[1,1,384]{2,1,0:T(1,128)S(1)} %reshape.158), channel_id=4, replica_groups=mesh['ctx'=16,'head'=32] {'head'}, dimensions={0}, use_global_device_ids=true | all-gather | bytes 50688 | tf_op jit(solution)/shard_map/all_gather | solution.py:29
  158.6 0.2 fusion.45
  158.9 1.2 while.31
  160.1 0.6 copy-done
  161.1 0.9 copy.117
  162.0 0.3 fusion.37
  162.2 0.3 fusion.31
  162.8 0.9 copy.118
  163.7 61.2 %all-gather.10.cloned.1.call-done = f32[32,128,128]{2,1,0:T(8,128)} async-done(((f32[2,128,128]{2,1,0:T(8,128)}), f32[32,128,128]{2,1,0:T(8,128)}) %all-gather.10.cloned.1.call-update) | async-done | bytes 2097168 | tf_op jit(solution)/shard_map/all_gather | solution.py:127
  224.9 3.8 %fusion.22 = f32[2,1,128,128]{3,1,2,0:T(1,128)S(1)} fusion(f32[16,2,1,1]{0,2,3,1:T(1,128)S(1)} %copy.125, f32[16,2,128,128]{3,2,1,0:T(8,128)} %bitcast.160), kind=kOutput, calls=%fused_computation.32 | convolution fusion | flops 6291456 | bytes 2228352 | tf_op jit(solution)/shard_map/nh,nhde->hde/dot_general | solution.py:23
  228.7 0.3 fusion.29
  229.0 0.3 fusion.26
  229.3 0.3 fusion.39
  229.6 0.9 copy.119
  230.5 0.3 fusion.40
  230.8 0.9 copy.120
  (85 shorter events, 4.4 us)
Async XLA Ops:
  7.2 53.4 %all-gather.8.cloned.1.call-start = ((), (), s32[]{:S(2)}) async-start(), calls=%async_computation | async-start | bytes 2228224 | tf_op jit(solution)/shard_map/all_gather | solution.py:69
  10.6 2.3 copy-start.3
  12.0 0.7 copy-start.1
  12.6 212.3 %all-gather.10.cloned.1.call-start = ((), (), s32[]{:S(2)}) async-start(), calls=%async_computation.1 | async-start | bytes 2228224 | tf_op jit(solution)/shard_map/all_gather | solution.py:127
  64.3 62.3 %copy-start.2 = (bf16[384,2,128]{2,1,0:T(2,128)(2,1)S(1)}, bf16[384,2,128]{2,1,0:T(2,128)(2,1)}, u32[]{:S(2)}) copy-start(bf16[384,2,128]{2,1,0:T(2,128)(2,1)} %param.15) | copy-start | bytes 589828
  64.4 62.3 %copy-start.4 = (f32[2,128]{1,0:T(2,128)S(1)}, f32[2,128]{1,0:T(2,128)}, u32[]{:S(2)}) copy-start(f32[2,128]{1,0:T(2,128)} %param.14) | copy-start | bytes 3076
  160.1 0.7 copy-start
Sparse Core Ops, SparseCore 0:
  12.8 47.7 all-gather.7
  160.9 63.9 all-gather.9
